TPU v7x, 32 devices: a whole 2x2x4 slice. The times are simulated.
32 devices in a mesh: dp: 8 (over z, x), expert: 4 (over y, core).
Axes of the slice: x: 2, y: 2, z: 4, core: 2. Of those that a mesh axis runs over, the one named last changes fastest.
Arguments:
- inputs: bfloat16 [32, 128, 2048], P(('dp', 'expert')), may hold values from -6 to 6
- cotangent: bfloat16 [32, 128, 2048], P(('dp', 'expert')), may hold values from -6 to 6
- lengths: int32 [32], P('dp'), may hold values from 1 to 128, 3072 in all
- dealing: int32 [8, 4], P('dp'), may hold values from 0 to 3, each once within a row
- routes: int32 [32, 128, 8], P(('dp', 'expert')), may hold values from 0 to 15, all different within a row; in each aligned block of 128 rows (0 to 127, 128 to 255, ..., all dimensions but the last counted through in order) at most 72 rows name the same one
- gate_values: float32 [32, 128, 8], P(('dp', 'expert')), may hold values from 0.25 to 0.75
- attn_gain: float32 [2048], replicated, may hold values from 0.1 to 1.9
- w_query: float32 [2048, 2048], P(('dp', 'expert')), may hold values from -0.125 to 0.125
- w_key: float32 [2048, 2048], P(('dp', 'expert')), may hold values from -0.125 to 0.125
- w_value: float32 [2048, 2048], P(('dp', 'expert')), may hold values from -0.125 to 0.125
- query_gain: float32 [2048], replicated, may hold values from 0.1 to 1.9
- key_gain: float32 [2048], replicated, may hold values from 0.1 to 1.9
- w_out: float32 [2048, 2048], P(('dp', 'expert')), may hold values from -0.5 to 0.5
- ffn_gain: float32 [2048], replicated, may hold values from 0.1 to 1.9
- w_gate: float32 [16, 2048, 1024], P('expert', 'dp'), may hold values from -0.125 to 0.125
- w_up: float32 [16, 2048, 1024], P('expert', 'dp'), may hold values from -0.125 to 0.125
- w_down: float32 [16, 1024, 2048], P('expert', 'dp'), may hold values from -0.1875 to 0.1875
Outputs:
- layer_out: bfloat16 [32, 128, 2048], P(('dp', 'expert'))
- grad_inputs: bfloat16 [32, 128, 2048], P(('dp', 'expert'))
- grad_attn_gain: float32 [2048], P(('dp', 'expert'))
- grad_w_query: float32 [2048, 2048], P(('dp', 'expert'))
- grad_w_key: float32 [2048, 2048], P(('dp', 'expert'))
- grad_w_value: float32 [2048, 2048], P(('dp', 'expert'))
- grad_query_gain: float32 [2048], P(('dp', 'expert'))
- grad_key_gain: float32 [2048], P(('dp', 'expert'))
- grad_w_out: float32 [2048, 2048], P(('dp', 'expert'))
- grad_ffn_gain: float32 [2048], P(('dp', 'expert'))
- grad_w_gate: float32 [16, 2048, 1024], P('expert', 'dp')
- grad_w_up: float32 [16, 2048, 1024], P('expert', 'dp')
- grad_w_down: float32 [16, 1024, 2048], P('expert', 'dp')
Inputs may be any that keep to these rules, and one draw needn't show every extreme that they name: `lengths`: the longest sequence has exactly 128 tokens. `dealing`: each row names every sequence of its group once. `routes`: each token names 8 different experts; within one dealt sequence no expert is named more than 72 times, and some sequence reaches 72 in every draw.
All inputs are finite; a program needn't handle non-finite values. No bound on the sum of `lengths` on one device may be relied on, other than what follows from the above.
Results may differ from a plain program's by a relative error of at most 0.015.
Values may be sent and summed in bfloat16 or wider, within the bound.
A program may use at most 384 MiB of HBM per device.

v0:
```python
import math
import jax
import jax.numpy as jnp
from jax import lax
from jax.sharding import PartitionSpec as P

HEADS = 16
epsilon = 1e-05


def norm_scale(values):
    return lax.rsqrt(jnp.mean(values * values, axis=-1, keepdims=True) + epsilon)


def norm_back(normed, row_scale, incoming):
    return row_scale * (incoming - normed * jnp.mean(incoming * normed, axis=-1, keepdims=True))


def angle_tables(length_rows, head_size):
    half_size = head_size // 2
    position = jnp.arange(length_rows, dtype=jnp.float32)[:, None]
    inverse = jnp.exp(
        jnp.arange(half_size, dtype=jnp.float32) * (-2.0 * math.log(10000.0) / head_size)
    )
    angles = position * inverse[None, :]
    return (jnp.cos(angles)[:, None, :], jnp.sin(angles)[:, None, :])


def rotate_pairs(values, cosine, sine_table):
    half_size = values.shape[-1] // 2
    first = values[..., :half_size]
    second = values[..., half_size:]
    return jnp.concatenate(
        [first * cosine - second * sine_table, second * cosine + first * sine_table], axis=-1
    )


def route_tables(expert_picks, experts, capacity):
    flat_picks = expert_picks.reshape(-1)
    onehot = (flat_picks[:, None] == jnp.arange(experts, dtype=jnp.int32)[None, :]).astype(
        jnp.int32
    )
    before = jnp.cumsum(onehot, axis=0) - onehot
    rank_within = jnp.sum(before * onehot, axis=1)
    slot_place = flat_picks * capacity + rank_within
    pair_count = flat_picks.shape[0]
    owner_pair = (
        jnp.zeros((experts * capacity,), jnp.int32)
        .at[slot_place]
        .set(jnp.arange(pair_count, dtype=jnp.int32))
    )
    filled = jnp.zeros((experts * capacity,), jnp.int32).at[slot_place].set(1)
    return (slot_place, owner_pair, filled)


def expert_front(received, gate_mat, up_mat):
    gate_pre = jnp.einsum("emd,edf->emf", received, gate_mat, preferred_element_type=jnp.float32)
    up_pre = jnp.einsum("emd,edf->emf", received, up_mat, preferred_element_type=jnp.float32)
    hidden_act = (jax.nn.silu(gate_pre) * up_pre).astype(jnp.bfloat16)
    return (gate_pre, up_pre, hidden_act)


def per_device(
    inputs,
    cotangent,
    lengths,
    dealing,
    routes,
    gate_values,
    attn_gain,
    w_query,
    w_key,
    w_value,
    query_gain,
    key_gain,
    w_out,
    ffn_gain,
    w_gate,
    w_up,
    w_down,
):
    group_size = lax.axis_size("expert")
    position = lax.axis_index("expert")
    deal_order = dealing[0]
    source = deal_order[position]
    dealt_rows = (
        lax.all_gather(inputs, "expert", axis=0, tiled=True),
        lax.all_gather(cotangent, "expert", axis=0, tiled=True),
    )
    seq_inputs = lax.dynamic_index_in_dim(dealt_rows[0], source, 0, keepdims=False).astype(
        jnp.float32
    )
    seq_grads = lax.dynamic_index_in_dim(dealt_rows[1], source, 0, keepdims=False).astype(
        jnp.float32
    )
    seq_length = lengths[source]
    length_rows, width = seq_inputs.shape
    head_size = width // HEADS
    attn_mats = (
        lax.all_gather(w_query.astype(jnp.bfloat16), ("dp", "expert"), axis=0, tiled=True),
        lax.all_gather(w_key.astype(jnp.bfloat16), ("dp", "expert"), axis=0, tiled=True),
        lax.all_gather(w_value.astype(jnp.bfloat16), ("dp", "expert"), axis=0, tiled=True),
        lax.all_gather(w_out.astype(jnp.bfloat16), ("dp", "expert"), axis=0, tiled=True),
    )
    query_mat, key_mat, value_mat, out_mat = attn_mats
    scale_in = norm_scale(seq_inputs)
    normed_in = seq_inputs * scale_in
    hidden_in = (normed_in * attn_gain).astype(jnp.bfloat16)
    query_raw = jnp.dot(hidden_in, query_mat, preferred_element_type=jnp.float32)
    key_raw = jnp.dot(hidden_in, key_mat, preferred_element_type=jnp.float32)
    values = jnp.dot(hidden_in, value_mat, preferred_element_type=jnp.float32).astype(jnp.bfloat16)
    cosine, sine_table = angle_tables(length_rows, head_size)
    query_scale = norm_scale(query_raw)
    query_normed = query_raw * query_scale
    key_scale = norm_scale(key_raw)
    key_normed = key_raw * key_scale
    queries = rotate_pairs(
        (query_normed * query_gain).reshape(length_rows, HEADS, head_size), cosine, sine_table
    ).astype(jnp.bfloat16)
    key_rows = rotate_pairs(
        (key_normed * key_gain).reshape(length_rows, HEADS, head_size), cosine, sine_table
    ).astype(jnp.bfloat16)
    head_values = values.reshape(length_rows, HEADS, head_size)
    factor = head_size ** (-0.5)
    row_index = jnp.arange(length_rows, dtype=jnp.int32)[:, None]
    col_index = jnp.arange(length_rows, dtype=jnp.int32)[None, :]
    visible = (col_index <= row_index) & (col_index < seq_length)
    scores = (
        jnp.einsum("ihd,jhd->hij", queries, key_rows, preferred_element_type=jnp.float32) * factor
    )
    scores = jnp.where(visible[None], scores, -1e30)
    weights = jax.nn.softmax(scores, axis=-1)
    weights_low = weights.astype(jnp.bfloat16)
    attended = jnp.einsum(
        "hij,jhd->ihd", weights_low, head_values, preferred_element_type=jnp.float32
    )
    attended = attended.reshape(length_rows, width).astype(jnp.bfloat16)
    residual = seq_inputs + jnp.dot(attended, out_mat, preferred_element_type=jnp.float32)
    scale_mid = norm_scale(residual)
    normed_mid = residual * scale_mid
    hidden_mid = (normed_mid * ffn_gain).astype(jnp.bfloat16)
    local_experts = w_gate.shape[0]
    experts = local_experts * group_size
    top_count = routes.shape[2]
    capacity = length_rows * top_count * 9 // (8 * experts)
    slot_place, owner_pair, filled = route_tables(routes[0], experts, capacity)
    live_slot = filled[:, None] > 0
    token_of_slot = owner_pair // top_count
    sending = jnp.where(live_slot, hidden_mid[token_of_slot], jnp.zeros((), jnp.bfloat16))
    sending = sending.reshape(group_size, local_experts, capacity, width)
    received = lax.all_to_all(sending, "expert", split_axis=0, concat_axis=2, tiled=True)[0]
    expert_mats = (
        lax.all_gather(w_gate.astype(jnp.bfloat16), "dp", axis=1, tiled=True),
        lax.all_gather(w_up.astype(jnp.bfloat16), "dp", axis=1, tiled=True),
        lax.all_gather(w_down.astype(jnp.bfloat16), "dp", axis=1, tiled=True),
    )
    gate_mat, up_mat, down_mat = expert_mats
    gate_pre, up_pre, hidden_act = expert_front(received, gate_mat, up_mat)
    expert_out = jnp.einsum(
        "emf,efd->emd", hidden_act, down_mat, preferred_element_type=jnp.float32
    ).astype(jnp.bfloat16)
    returned = lax.all_to_all(
        expert_out[None], "expert", split_axis=2, concat_axis=0, tiled=True
    ).reshape(experts * capacity, width)
    picked = returned[slot_place].reshape(length_rows, top_count, width)
    mixture = jnp.sum(gate_values[0][:, :, None] * picked.astype(jnp.float32), axis=1)
    layer_rows = (residual + mixture).astype(jnp.bfloat16)
    flat_gates = gate_values[0].reshape(-1)
    slot_grads = jnp.where(
        live_slot, flat_gates[owner_pair][:, None] * seq_grads[token_of_slot], 0.0
    ).astype(jnp.bfloat16)
    slot_grads = slot_grads.reshape(group_size, local_experts, capacity, width)
    out_grads = lax.all_to_all(slot_grads, "expert", split_axis=0, concat_axis=2, tiled=True)[0]
    gate_mat, up_mat, down_mat = (
        lax.all_gather(w_gate.astype(jnp.bfloat16), "dp", axis=1, tiled=True),
        lax.all_gather(w_up.astype(jnp.bfloat16), "dp", axis=1, tiled=True),
        lax.all_gather(w_down.astype(jnp.bfloat16), "dp", axis=1, tiled=True),
    )
    grad_hidden = jnp.einsum(
        "emd,efd->emf", out_grads, down_mat, preferred_element_type=jnp.float32
    )
    sigmoid_gate = jax.nn.sigmoid(gate_pre)
    grad_gate_pre = (
        grad_hidden * up_pre * sigmoid_gate * (1.0 + gate_pre * (1.0 - sigmoid_gate))
    ).astype(jnp.bfloat16)
    grad_up_pre = (grad_hidden * gate_pre * sigmoid_gate).astype(jnp.bfloat16)
    grad_slots = jnp.einsum(
        "emf,edf->emd", grad_gate_pre, gate_mat, preferred_element_type=jnp.float32
    )
    grad_slots = (
        grad_slots
        + jnp.einsum("emf,edf->emd", grad_up_pre, up_mat, preferred_element_type=jnp.float32)
    ).astype(jnp.bfloat16)
    grad_down = jnp.einsum(
        "emf,emd->efd", hidden_act, out_grads, preferred_element_type=jnp.float32
    )
    grad_gate = jnp.einsum(
        "emd,emf->edf", received, grad_gate_pre, preferred_element_type=jnp.float32
    )
    grad_up = jnp.einsum("emd,emf->edf", received, grad_up_pre, preferred_element_type=jnp.float32)
    expert_summed = (
        lax.psum_scatter(
            grad_gate.astype(jnp.bfloat16), "dp", scatter_dimension=1, tiled=True
        ).astype(jnp.float32),
        lax.psum_scatter(
            grad_up.astype(jnp.bfloat16), "dp", scatter_dimension=1, tiled=True
        ).astype(jnp.float32),
        lax.psum_scatter(
            grad_down.astype(jnp.bfloat16), "dp", scatter_dimension=1, tiled=True
        ).astype(jnp.float32),
    )
    sent_back = lax.all_to_all(
        grad_slots[None], "expert", split_axis=2, concat_axis=0, tiled=True
    ).reshape(experts * capacity, width)
    grad_mid = jnp.sum(
        sent_back[slot_place].reshape(length_rows, top_count, width).astype(jnp.float32), axis=1
    )
    ffn_gain_part = jnp.sum(grad_mid * normed_mid, axis=0)
    grad_resid = seq_grads + norm_back(normed_mid, scale_mid, grad_mid * ffn_gain)
    resid_low = grad_resid.astype(jnp.bfloat16)
    grad_out_mat = jnp.einsum("td,te->de", attended, resid_low, preferred_element_type=jnp.float32)
    grad_attended = jnp.einsum(
        "te,de->td", resid_low, out_mat, preferred_element_type=jnp.float32
    ).astype(jnp.bfloat16)
    grad_attended = grad_attended.reshape(length_rows, HEADS, head_size)
    grad_values = jnp.einsum(
        "hij,ihd->jhd", weights_low, grad_attended, preferred_element_type=jnp.float32
    )
    grad_values = grad_values.reshape(length_rows, width).astype(jnp.bfloat16)
    grad_weights = jnp.einsum(
        "ihd,jhd->hij", grad_attended, head_values, preferred_element_type=jnp.float32
    )
    grad_scores = (
        weights * (grad_weights - jnp.sum(weights * grad_weights, axis=-1, keepdims=True))
    ).astype(jnp.bfloat16)
    grad_queries = (
        jnp.einsum("hij,jhd->ihd", grad_scores, key_rows, preferred_element_type=jnp.float32)
        * factor
    )
    grad_keys = (
        jnp.einsum("hij,ihd->jhd", grad_scores, queries, preferred_element_type=jnp.float32)
        * factor
    )
    query_turned = rotate_pairs(grad_queries, cosine, -sine_table).reshape(length_rows, width)
    key_turned = rotate_pairs(grad_keys, cosine, -sine_table).reshape(length_rows, width)
    query_gain_part = jnp.sum(query_turned * query_normed, axis=0)
    key_gain_part = jnp.sum(key_turned * key_normed, axis=0)
    grad_query_raw = norm_back(query_normed, query_scale, query_turned * query_gain).astype(
        jnp.bfloat16
    )
    grad_key_raw = norm_back(key_normed, key_scale, key_turned * key_gain).astype(jnp.bfloat16)
    grad_query_mat = jnp.einsum(
        "td,te->de", hidden_in, grad_query_raw, preferred_element_type=jnp.float32
    )
    grad_key_mat = jnp.einsum(
        "td,te->de", hidden_in, grad_key_raw, preferred_element_type=jnp.float32
    )
    grad_value_mat = jnp.einsum(
        "td,te->de", hidden_in, grad_values, preferred_element_type=jnp.float32
    )
    grad_hidden_in = jnp.einsum(
        "te,de->td", grad_query_raw, query_mat, preferred_element_type=jnp.float32
    )
    grad_hidden_in = grad_hidden_in + jnp.einsum(
        "te,de->td", grad_key_raw, key_mat, preferred_element_type=jnp.float32
    )
    grad_hidden_in = grad_hidden_in + jnp.einsum(
        "te,de->td", grad_values, value_mat, preferred_element_type=jnp.float32
    )
    attn_gain_part = jnp.sum(grad_hidden_in * normed_in, axis=0)
    grad_seq = grad_resid + norm_back(normed_in, scale_in, grad_hidden_in * attn_gain)
    attn_summed = (
        lax.psum_scatter(grad_query_mat, ("dp", "expert"), scatter_dimension=0, tiled=True),
        lax.psum_scatter(grad_key_mat, ("dp", "expert"), scatter_dimension=0, tiled=True),
        lax.psum_scatter(grad_value_mat, ("dp", "expert"), scatter_dimension=0, tiled=True),
        lax.psum_scatter(grad_out_mat, ("dp", "expert"), scatter_dimension=0, tiled=True),
        lax.psum_scatter(attn_gain_part, ("dp", "expert"), scatter_dimension=0, tiled=True),
        lax.psum_scatter(query_gain_part, ("dp", "expert"), scatter_dimension=0, tiled=True),
        lax.psum_scatter(key_gain_part, ("dp", "expert"), scatter_dimension=0, tiled=True),
        lax.psum_scatter(ffn_gain_part, ("dp", "expert"), scatter_dimension=0, tiled=True),
    )
    back_rows = (
        lax.all_gather(layer_rows[None], "expert", axis=0, tiled=True),
        lax.all_gather(grad_seq.astype(jnp.bfloat16)[None], "expert", axis=0, tiled=True),
    )
    holder = jnp.sum(jnp.where(deal_order == position, jnp.arange(group_size, dtype=jnp.int32), 0))
    out_rows = lax.dynamic_slice_in_dim(back_rows[0], holder, 1, 0)
    grad_rows_out = lax.dynamic_slice_in_dim(back_rows[1], holder, 1, 0)
    return (
        out_rows,
        grad_rows_out,
        attn_summed[4],
        attn_summed[0],
        attn_summed[1],
        attn_summed[2],
        attn_summed[5],
        attn_summed[6],
        attn_summed[3],
        attn_summed[7],
        expert_summed[0],
        expert_summed[1],
        expert_summed[2],
    )


def solution(mesh):
    return jax.shard_map(
        per_device,
        mesh=mesh,
        in_specs=(
            P(("dp", "expert"), None, None),
            P(("dp", "expert"), None, None),
            P("dp"),
            P("dp", None),
            P(("dp", "expert"), None, None),
            P(("dp", "expert"), None, None),
            P(),
            P(("dp", "expert"), None),
            P(("dp", "expert"), None),
            P(("dp", "expert"), None),
            P(),
            P(),
            P(("dp", "expert"), None),
            P(),
            P("expert", "dp", None),
            P("expert", "dp", None),
            P("expert", "dp", None),
        ),
        out_specs=(
            P(("dp", "expert"), None, None),
            P(("dp", "expert"), None, None),
            P(("dp", "expert")),
            P(("dp", "expert"), None),
            P(("dp", "expert"), None),
            P(("dp", "expert"), None),
            P(("dp", "expert")),
            P(("dp", "expert")),
            P(("dp", "expert"), None),
            P(("dp", "expert")),
            P("expert", "dp", None),
            P("expert", "dp", None),
            P("expert", "dp", None),
        ),
        check_vma=False,
    )
```

profile of v0, /device:TPU:3, one launch (start us, length us, event | category | flops | bytes accessed | tf_op | source)
XLA Modules:
  0.0 2965.7 jit_solution(5224413650591121145)
XLA Ops:
  53.2 6.7 gather_fusion.3
  60.0 6.8 select_convert_fusion
  66.8 6.3 all-to-all-start.2
  74.4 81.8 %all-gather.20.cloned.1.call-done = bf16[2048,2048]{1,0:T(8,128)(2,1)} async-done(((bf16[64,2048]{1,0:T(8,128)(2,1)}), bf16[2048,2048]{1,0:T(8,128)(2,1)}) %all-gather.20.cloned.1.call-update) | async-done | bytes 8388624 | tf_op jit(solution)/shard_map/all_gather | solution.py:101
  162.5 73.0 %all-gather.18.cloned.1.call-done = bf16[2048,2048]{1,0:T(8,128)(2,1)} async-done(((bf16[64,2048]{1,0:T(8,128)(2,1)}), bf16[2048,2048]{1,0:T(8,128)(2,1)}) %all-gather.18.cloned.1.call-update) | async-done | bytes 8388624 | tf_op jit(solution)/shard_map/all_gather | solution.py:100
  248.1 66.8 %all-gather.16.cloned.1.call-done = bf16[2048,2048]{1,0:T(8,128)(2,1)} async-done(((bf16[64,2048]{1,0:T(8,128)(2,1)}), bf16[2048,2048]{1,0:T(8,128)(2,1)}) %all-gather.16.cloned.1.call-update) | async-done | bytes 8388624 | tf_op jit(solution)/shard_map/all_gather | solution.py:102
  314.9 5.5 fusion.14
  322.9 71.5 %all-gather.22.cloned.1.call-done = bf16[2048,2048]{1,0:T(8,128)(2,1)} async-done(((bf16[64,2048]{1,0:T(8,128)(2,1)}), bf16[2048,2048]{1,0:T(8,128)(2,1)}) %all-gather.22.cloned.1.call-update) | async-done | bytes 8388624 | tf_op jit(solution)/shard_map/all_gather | solution.py:103
  399.4 6.0 gather_fusion
  405.4 5.4 broadcast_select_fusion
  416.1 5.4 copy.102
  421.5 47.6 %all-to-all-done = bf16[4,4,72,2048]{3,2,1,0:T(8,128)(2,1)} async-done(((bf16[4,4,72,2048]{3,2,1,0:T(8,128)(2,1)}), bf16[4,4,72,2048]{3,2,1,0:T(8,128)(2,1)}, u32[]{:S(2)}, u32[]{:S(2)}) %all-to-all-start) | async-done | bytes 4718624 | tf_op jit(solution)/shard_map/all_to_all | solution.py:151
  474.4 147.3 %all-gather.24.cloned.1.call-done = bf16[4,2048,1024]{2,1,0:T(8,128)(2,1)} async-done(((bf16[4,256,1024]{2,1,0:T(8,128)(2,1)}), bf16[4,2048,1024]{2,1,0:T(8,128)(2,1)}) %all-gather.24.cloned.1.call-update) | async-done | bytes 16777232 | tf_op jit(solution)/shard_map/all_gather | solution.py:153
  621.7 13.3 fusion.79
  634.9 215.3 %all-gather.26.cloned.1.call-done = bf16[4,2048,1024]{2,1,0:T(8,128)(2,1)} async-done(((bf16[4,256,1024]{2,1,0:T(8,128)(2,1)}), bf16[4,2048,1024]{2,1,0:T(8,128)(2,1)}) %all-gather.26.cloned.1.call-update) | async-done | bytes 16777232 | tf_op jit(solution)/shard_map/all_gather | solution.py:154
  850.2 13.2 fusion.80
  863.4 215.4 %all-gather.28.cloned.1.call-done = bf16[4,1024,2048]{2,1,0:T(8,128)(2,1)} async-done(((bf16[4,128,2048]{2,1,0:T(8,128)(2,1)}), bf16[4,1024,2048]{2,1,0:T(8,128)(2,1)}) %all-gather.28.cloned.1.call-update) | async-done | bytes 16777232 | tf_op jit(solution)/shard_map/all_gather | solution.py:155
  1078.8 15.1 multiply_convert_fusion
  1093.9 11.5 fusion.81
  1105.4 13.6 fusion.2
  1119.0 8.1 copy.103
  1127.2 6.4 all-to-all-start.3
  1133.6 11.5 convert_bitcast_fusion
  1145.0 5.8 copy.99
  1150.8 35.7 %all-to-all-done.3 = bf16[1,4,288,2048]{3,1,0,2:T(4,128)(2,1)} async-done(((bf16[1,4,288,2048]{3,1,0,2:T(4,128)(2,1)}), bf16[1,4,288,2048]{3,1,0,2:T(4,128)(2,1)}, u32[]{:S(2)}, u32[]{:S(2)}) %all-to-all-start.3) | async-done | bytes 4718624 | tf_op jit(solution)/shard_map/all_to_all | solution.py:212
  1186.6 5.8 all-to-all-start.1
  1192.5 7.2 copy.104
  1199.6 11.9 gather_fusion.4
  1216.9 28.4 all-to-all-done.1
  1245.4 7.1 copy.100
  1252.5 11.9 gather_fusion.1
  1264.4 6.5 fusion.1
  1273.2 7.2 convolution_convert_fusion.3
  1304.9 14.7 convolution_convert_fusion.2
  1319.7 14.9 convolution_convert_fusion.1
  1334.7 15.5 convolution_convert_fusion
  1350.3 9.1 fusion.37
  1360.4 8.2 fusion.28
  1369.7 8.3 fusion.67
  1379.0 8.3 fusion.69
  1390.5 42.1 %all-reduce.4 = (f32[2048]{0:T(1024)S(1)}, f32[2048]{0:T(1024)S(1)}, f32[2048]{0:T(1024)S(1)}, f32[2048]{0:T(1024)S(1)}) all-reduce(f32[2048]{0:T(1024)S(1)} %get-tuple-element.13, f32[2048]{0:T(1024)S(1)} %get-tuple-element.19, f32[2048]{0:T(1024)S(1)} %get-tuple-element.17, ...), channel_id=4, replica_groups=mesh['dp'=8,'expert'=4] {'dp','expert'}, use_global_device_ids=true, to_apply=%region_20.21.clone | all-reduce | flops 8192 | bytes 65536
  1438.8 198.7 %reduce-scatter.16.cloned.1.call-done = bf16[4,256,1024]{2,1,0:T(8,128)(2,1)} async-done(((bf16[4,2048,1024]{2,1,0:T(8,128)(2,1)}), bf16[4,256,1024]{2,1,0:T(8,128)(2,1)}) %reduce-scatter.16.cloned.1.call-update) | async-done | bytes 2097168 | tf_op jit(solution)/shard_map/reduce_scatter | solution.py:202
  1641.5 281.9 %reduce-scatter.18.cloned.1.call-done = bf16[4,256,1024]{2,1,0:T(8,128)(2,1)} async-done(((bf16[4,2048,1024]{2,1,0:T(8,128)(2,1)}), bf16[4,256,1024]{2,1,0:T(8,128)(2,1)}) %reduce-scatter.18.cloned.1.call-update) | async-done | bytes 2097168 | tf_op jit(solution)/shard_map/reduce_scatter | solution.py:205
  1927.5 281.3 %reduce-scatter.20.cloned.1.call-done = bf16[4,128,2048]{2,1,0:T(8,128)(2,1)} async-done(((bf16[4,1024,2048]{2,1,0:T(8,128)(2,1)}), bf16[4,128,2048]{2,1,0:T(8,128)(2,1)}) %reduce-scatter.20.cloned.1.call-update) | async-done | bytes 2097168 | tf_op jit(solution)/shard_map/reduce_scatter | solution.py:208
  2213.0 183.3 %reduce-scatter.14.cloned.1.call-done = f32[64,2048]{1,0:T(8,128)} async-done(((f32[2048,2048]{1,0:T(8,128)}), f32[64,2048]{1,0:T(8,128)}) %reduce-scatter.14.cloned.1.call-update) | async-done | bytes 524304 | tf_op jit(solution)/shard_map/reduce_scatter | solution.py:276
  2396.3 187.4 %reduce-scatter.12.cloned.1.call-done = f32[64,2048]{1,0:T(8,128)} async-done(((f32[2048,2048]{1,0:T(8,128)}), f32[64,2048]{1,0:T(8,128)}) %reduce-scatter.12.cloned.1.call-update) | async-done | bytes 524304 | tf_op jit(solution)/shard_map/reduce_scatter | solution.py:275
  2583.8 186.7 %reduce-scatter.10.cloned.1.call-done = f32[64,2048]{1,0:T(8,128)} async-done(((f32[2048,2048]{1,0:T(8,128)}), f32[64,2048]{1,0:T(8,128)}) %reduce-scatter.10.cloned.1.call-update) | async-done | bytes 524304 | tf_op jit(solution)/shard_map/reduce_scatter | solution.py:274
  2770.5 188.1 %reduce-scatter.8.cloned.1.call-done = f32[64,2048]{1,0:T(8,128)} async-done(((f32[2048,2048]{1,0:T(8,128)}), f32[64,2048]{1,0:T(8,128)}) %reduce-scatter.8.cloned.1.call-update) | async-done | bytes 524304 | tf_op jit(solution)/shard_map/reduce_scatter | solution.py:273
  (246 shorter events, 136.6 us)
Async XLA Ops:
  7.2 44.9 %all-gather.30.cloned.1.call-start = ((), (), s32[]{:S(2)}) async-start(), calls=%async_computation.19 | async-start | bytes 2621440 | tf_op jit(solution)/shard_map/all_gather | solution.py:88
  7.9 65.2 %all-gather.14.cloned.1.call-start = ((), (), s32[]{:S(2)}) async-start(), calls=%async_computation.11 | async-start | bytes 2621440 | tf_op jit(solution)/shard_map/all_gather | solution.py:87
  8.7 147.5 %all-gather.20.cloned.1.call-start = ((), (), s32[]{:S(2)}) async-start(), calls=%async_computation.14 | async-start | bytes 8650752 | tf_op jit(solution)/shard_map/all_gather | solution.py:101
  10.5 225.0 %all-gather.18.cloned.1.call-start = ((), (), s32[]{:S(2)}) async-start(), calls=%async_computation.13 | async-start | bytes 8650752 | tf_op jit(solution)/shard_map/all_gather | solution.py:100
  12.4 302.6 %all-gather.16.cloned.1.call-start = ((), (), s32[]{:S(2)}) async-start(), calls=%async_computation.12 | async-start | bytes 8650752 | tf_op jit(solution)/shard_map/all_gather | solution.py:102
  14.2 380.2 %all-gather.22.cloned.1.call-start = ((), (), s32[]{:S(2)}) async-start(), calls=%async_computation.15 | async-start | bytes 8650752 | tf_op jit(solution)/shard_map/all_gather | solution.py:103
  16.1 605.6 %all-gather.24.cloned.1.call-start = ((), (), s32[]{:S(2)}) async-start(), calls=%async_computation.16 | async-start | bytes 18874368 | tf_op jit(solution)/shard_map/all_gather | solution.py:153
  20.2 830.1 %all-gather.26.cloned.1.call-start = ((), (), s32[]{:S(2)}) async-start(), calls=%async_computation.17 | async-start | bytes 18874368 | tf_op jit(solution)/shard_map/all_gather | solution.py:154
  24.1 5.8 copy-start.34
  24.1 20.1 copy-start.32
  24.1 1054.7 %all-gather.28.cloned.1.call-start = ((), (), s32[]{:S(2)}) async-start(), calls=%async_computation.18 | async-start | bytes 18874368 | tf_op jit(solution)/shard_map/all_gather | solution.py:155
  30.2 19.6 copy-start.44
  35.4 16.6 copy-start.35
  51.2 269.3 %copy-start.37 = (pred[128,128]{0,1:T(8,128)(4,1)}, pred[128,128]{0,1:T(8,128)(4,1)S(1)}, u32[]{:S(2)}) copy-start(pred[128,128]{0,1:T(8,128)(4,1)S(1)} %fusion.48) | copy-start | bytes 49156
  52.1 190.2 %copy-start.22 = (f32[128,64]{1,0:T(8,128)}, f32[128,64]{1,0:T(8,128)S(1)}, u32[]{:S(2)}) copy-start(f32[128,64]{1,0:T(8,128)S(1)} %get-tuple-element.50) | copy-start | bytes 98308
  66.8 89.4 %copy-start.11 = (f32[2048]{0:T(1024)S(1)}, f32[2048]{0:T(1024)}, u32[]{:S(2)}) copy-start(f32[2048]{0:T(1024)} %param.23) | copy-start | bytes 24580
  66.8 344.0 %all-to-all-start.2 = ((bf16[4,4,72,2048]{3,2,1,0:T(8,128)(2,1)}), bf16[4,4,72,2048]{3,2,1,0:T(8,128)(2,1)}, u32[]{:S(2)}, u32[]{:S(2)}) async-start(bf16[4,4,72,2048]{3,2,1,0:T(8,128)(2,1)} %select_convert_fusion), calls=%async_computation.2 | async-start | bytes 9437184 | tf_op jit(solution)/shard_map/all_to_all | solution.py:173
  74.4 240.6 %copy-start.25 = (f32[128]{0:T(128)}, f32[128]{0:T(128)S(1)}, u32[]{:S(2)}) copy-start(f32[128]{0:T(128)S(1)} %add_rsqrt_fusion.3) | copy-start | bytes 1540
  74.4 87.8 %copy-start.28 = (f32[2048]{0:T(1024)S(1)}, f32[2048]{0:T(1024)}, u32[]{:S(2)}) copy-start(f32[2048]{0:T(1024)} %param.28) | copy-start | bytes 24580
  74.4 161.1 %copy-start.4 = (bf16[4,128,2048]{2,1,0:T(8,128)(2,1)S(1)}, bf16[4,128,2048]{2,1,0:T(8,128)(2,1)}, u32[]{:S(2)}) copy-start(bf16[4,128,2048]{2,1,0:T(8,128)(2,1)} %all-gather.14.cloned.1.call-done) | copy-start | bytes 6291460
  162.5 78.8 %copy-start.30 = (f32[2048]{0:T(1024)S(1)}, f32[2048]{0:T(1024)}, u32[]{:S(2)}) copy-start(f32[2048]{0:T(1024)} %param.27) | copy-start | bytes 24580
  244.6 75.8 %copy-start.13 = (bf16[128,16,64]{2,0,1:T(8,128)(2,1)}, bf16[128,16,64]{2,0,1:T(8,128)(2,1)S(1)}, u32[]{:S(2)}) copy-start(bf16[128,16,64]{2,0,1:T(8,128)(2,1)S(1)} %get-tuple-element.28) | copy-start | bytes 786436
  244.6 75.8 %copy-start.15 = (bf16[128,16,64]{2,0,1:T(8,128)(2,1)}, bf16[128,16,64]{2,0,1:T(8,128)(2,1)S(1)}, u32[]{:S(2)}) copy-start(bf16[128,16,64]{2,0,1:T(8,128)(2,1)S(1)} %get-tuple-element.29) | copy-start | bytes 786436
  248.1 72.3 %copy-start.38 = (f32[16,128]{1,0:T(8,128)}, f32[16,128]{1,0:T(8,128)S(1)}, u32[]{:S(2)}) copy-start(f32[16,128]{1,0:T(8,128)S(1)} %get-tuple-element.55) | copy-start | bytes 24580
  322.9 76.3 %copy-start.10 = (bf16[16,128,128]{2,1,0:T(8,128)(2,1)}, bf16[16,128,128]{2,1,0:T(8,128)(2,1)S(1)}, u32[]{:S(2)}) copy-start(bf16[16,128,128]{2,1,0:T(8,128)(2,1)S(1)} %convolution_convert_fusion.6) | copy-start | bytes 1572868
  410.8 58.3 %all-to-all-start = ((bf16[4,4,72,2048]{3,2,1,0:T(8,128)(2,1)}), bf16[4,4,72,2048]{3,2,1,0:T(8,128)(2,1)}, u32[]{:S(2)}, u32[]{:S(2)}) async-start(bf16[4,4,72,2048]{3,2,1,0:T(8,128)(2,1)} %broadcast_select_fusion), calls=%async_computation | async-start | bytes 9437184 | tf_op jit(solution)/shard_map/all_to_all | solution.py:151
  1127.2 59.4 %all-to-all-start.3 = ((bf16[1,4,288,2048]{3,1,0,2:T(4,128)(2,1)}), bf16[1,4,288,2048]{3,1,0,2:T(4,128)(2,1)}, u32[]{:S(2)}, u32[]{:S(2)}) async-start(bf16[1,4,288,2048]{3,1,0,2:T(4,128)(2,1)} %copy.103), calls=%async_computation.3 | async-start | bytes 9437184 | tf_op jit(solution)/shard_map/all_to_all | solution.py:212
  1150.8 41.5 %copy-start.33 = (f32[1,128,8]{1,2,0:T(8,128)S(1)}, f32[1,128,8]{1,2,0:T(8,128)}, u32[]{:S(2)}) copy-start(f32[1,128,8]{1,2,0:T(8,128)} %param.22) | copy-start | bytes 12292
  1150.8 41.6 %copy-start.36 = (s32[1024,1]{0,1:T(1,128)S(1)}, s32[1024,1]{0,1:T(1,128)}, u32[]{:S(2)}) copy-start(s32[1024,1]{0,1:T(1,128)} %copy-done.35) | copy-start | bytes 12292
  1186.6 58.8 %all-to-all-start.1 = ((bf16[1,4,288,2048]{3,1,0,2:T(4,128)(2,1)}), bf16[1,4,288,2048]{3,1,0,2:T(4,128)(2,1)}, u32[]{:S(2)}, u32[]{:S(2)}) async-start(bf16[1,4,288,2048]{3,1,0,2:T(4,128)(2,1)} %copy.99), calls=%async_computation.1 | async-start | bytes 9437184 | tf_op jit(solution)/shard_map/all_to_all | solution.py:162
  1192.4 242.6 %all-gather.34.cloned.1.call-start = ((), (), s32[]{:S(2)}) async-start(), calls=%async_computation.28 | async-start | bytes 2621440 | tf_op jit(solution)/shard_map/all_gather | solution.py:284
  1273.2 9.3 copy-start.14
  1273.2 9.3 copy-start.16
  1273.2 9.3 copy-start.17
  1273.2 9.3 copy-start.18
  1273.2 9.3 copy-start.39
  1288.8 5.0 slice-start.2
  1291.0 5.7 copy-start.8
  1291.5 5.2 slice-start
  1293.8 5.9 slice-start.4
  1304.1 132.8 %all-gather.32.cloned.1.call-start = ((), (), s32[]{:S(2)}) async-start(), calls=%async_computation.27 | async-start | bytes 2621440 | tf_op jit(solution)/shard_map/all_gather | solution.py:283
  1304.8 332.6 %reduce-scatter.16.cloned.1.call-start = ((), (), s32[]{:S(2)}) async-start(), calls=%async_computation.24 | async-start | bytes 18874368 | tf_op jit(solution)/shard_map/reduce_scatter | solution.py:202
  1319.7 603.8 %reduce-scatter.18.cloned.1.call-start = ((), (), s32[]{:S(2)}) async-start(), calls=%async_computation.25 | async-start | bytes 18874368 | tf_op jit(solution)/shard_map/reduce_scatter | solution.py:205
  1334.7 874.2 %reduce-scatter.20.cloned.1.call-start = ((), (), s32[]{:S(2)}) async-start(), calls=%async_computation.26 | async-start | bytes 18874368 | tf_op jit(solution)/shard_map/reduce_scatter | solution.py:208
  1350.2 1046.1 %reduce-scatter.14.cloned.1.call-start = ((), (), s32[]{:S(2)}) async-start(), calls=%async_computation.23 | async-start | bytes 17301504 | tf_op jit(solution)/shard_map/reduce_scatter | solution.py:276
  1359.4 1224.3 %reduce-scatter.12.cloned.1.call-start = ((), (), s32[]{:S(2)}) async-start(), calls=%async_computation.22 | async-start | bytes 17301504 | tf_op jit(solution)/shard_map/reduce_scatter | solution.py:275
  1368.7 1401.8 %reduce-scatter.10.cloned.1.call-start = ((), (), s32[]{:S(2)}) async-start(), calls=%async_computation.21 | async-start | bytes 17301504 | tf_op jit(solution)/shard_map/reduce_scatter | solution.py:274
  1378.0 1580.6 %reduce-scatter.8.cloned.1.call-start = ((), (), s32[]{:S(2)}) async-start(), calls=%async_computation.20 | async-start | bytes 17301504 | tf_op jit(solution)/shard_map/reduce_scatter | solution.py:273
  (27 other events, 52.7 us)
Sparse Core Ops, SparseCore 0:
  9.6 24.2 all-gather.29
  35.4 22.6 all-gather.13
  61.5 94.6 all-gather.19
  159.5 75.9 all-gather.17
  238.8 76.1 all-gather.15
  318.2 76.1 all-gather.21
  397.2 224.4 all-gather.23
  624.4 225.7 all-gather.25
  853.0 225.7 all-gather.27
  1304.2 21.3 all-gather.33
  1327.8 22.5 all-gather.31
  1354.1 283.3 reduce-scatter.15
  1641.7 281.6 reduce-scatter.17
  1927.1 281.7 reduce-scatter.19
  2211.7 184.6 reduce-scatter.13
  2399.2 184.5 reduce-scatter.11
  2586.6 183.8 reduce-scatter.9
  2773.3 185.2 reduce-scatter.7
where the time goes:
time: 2970 us
  waiting for transfers between devices  2490 us (84%)
  matrix products  205 us (7%)
  local copies, waits for them, and re-layouts  107 us (4%)
  other arithmetic  74.5 us (3%)
  blocking collectives  42.1 us (1%)
    reduce_scatter x1, waiting for transfers between devices, per_device(): lax.psum_scatter(grad_up.astype(jnp.bfloat16), 'dp', scatter_dimension=1,...  282 us
    reduce_scatter x1, waiting for transfers between devices, per_device(): lax.psum_scatter(grad_down.astype(jnp.bfloat16), 'dp', scatter_dimension=...  281 us
    all_gather x1, waiting for transfers between devices, per_device(): lax.all_gather(w_down.astype(jnp.bfloat16), 'dp', axis=1, tiled=True)  215 us
    all_gather x1, waiting for transfers between devices, per_device(): lax.all_gather(w_up.astype(jnp.bfloat16), 'dp', axis=1, tiled=True)  215 us
    reduce_scatter x1, waiting for transfers between devices, per_device(): lax.psum_scatter(grad_gate.astype(jnp.bfloat16), 'dp', scatter_dimension=...  199 us
    reduce_scatter x1, waiting for transfers between devices, per_device(): lax.psum_scatter(grad_query_mat, ('dp', 'expert'), scatter_dimension=0, t...  188 us
    reduce_scatter x1, waiting for transfers between devices, per_device(): lax.psum_scatter(grad_value_mat, ('dp', 'expert'), scatter_dimension=0, t...  187 us
    reduce_scatter x1, waiting for transfers between devices, per_device(): lax.psum_scatter(grad_key_mat, ('dp', 'expert'), scatter_dimension=0, til...  187 us
  transfers between devices with their start and end apart: 22, of which 17 were waited for; matrix products, arithmetic and copies ran while one was open for 9% of the time, Pallas kernels for 0%

commit v1 on v0

--- a/solution.py
+++ b/solution.py
@@ -6,6 +6,24 @@
 
 HEADS = 16
 epsilon = 1e-05
+
+
+def ring_gather(array, axis, dim):
+    ways, here, step = (lax.axis_size(axis), lax.axis_index(axis), array.shape[dim])
+    dims = [n * ways if d == dim else n for d, n in enumerate(array.shape)]
+    full = lax.dynamic_update_slice_in_dim(
+        jnp.zeros(dims, array.dtype), array, here * step, axis=dim
+    )
+    going_up = going_down = array
+    for far in range(1, ways // 2 + 1):
+        going_up = lax.ppermute(going_up, axis, [(d, (d + 1) % ways) for d in range(ways)])
+        full = lax.dynamic_update_slice_in_dim(full, going_up, (here - far) % ways * step, axis=dim)
+        if 2 * far < ways:
+            going_down = lax.ppermute(going_down, axis, [(d, (d - 1) % ways) for d in range(ways)])
+            full = lax.dynamic_update_slice_in_dim(
+                full, going_down, (here + far) % ways * step, axis=dim
+            )
+    return full
 
 
 def norm_scale(values):
@@ -151,7 +169,7 @@
     received = lax.all_to_all(sending, "expert", split_axis=0, concat_axis=2, tiled=True)[0]
     expert_mats = (
         lax.all_gather(w_gate.astype(jnp.bfloat16), "dp", axis=1, tiled=True),
-        lax.all_gather(w_up.astype(jnp.bfloat16), "dp", axis=1, tiled=True),
+        ring_gather(w_up.astype(jnp.bfloat16), "dp", 1),
         lax.all_gather(w_down.astype(jnp.bfloat16), "dp", axis=1, tiled=True),
     )
     gate_mat, up_mat, down_mat = expert_mats

time: 2970 us -> 3080 us (1.037)
  waiting for transfers between devices: 2490 us -> 2560 us
    ppermute x0 -> x7, waiting for transfers between devices: none -> 242 us  [the longest x4 155 us: ring_gather(): lax.ppermute(going_up, axis, [(d, (d + 1) % ways) for d in range(ways)])]
    all_gather x1, waiting for transfers between devices: 73 us -> 0.01 us  [per_device(): lax.all_gather(w_query.astype(jnp.bfloat16), ('dp', 'expert'), axis=0, ti...]
    all_to_all x1, waiting for transfers between devices: 47.6 us -> 0.01 us  [per_device(): lax.all_to_all(sending, 'expert', split_axis=0, concat_axis=2, tiled=True)]
  transfers between devices with their start and end apart: 22 -> 29, of which waited for: 17 -> 18; matrix products, arithmetic and copies ran while one was open for 9% -> 11% of each run, Pallas kernels for 0% -> 0%
where the time goes in v1:
time: 3080 us; the launch traced here: 3070 us
  waiting for transfers between devices  2560 us (83%)
  matrix products  206 us (7%)
  local copies, waits for them, and re-layouts  136 us (4%)
  other arithmetic  73 us (2%)
  blocking collectives  42.2 us (1%)
  starting transfers between devices  34.5 us (1%)
    reduce_scatter x1, waiting for transfers between devices, per_device(): lax.psum_scatter(grad_up.astype(jnp.bfloat16), 'dp', scatter_dimension=1,...  282 us
    reduce_scatter x1, waiting for transfers between devices, per_device(): lax.psum_scatter(grad_down.astype(jnp.bfloat16), 'dp', scatter_dimension=...  281 us
    all_gather x1, waiting for transfers between devices, per_device(): lax.all_gather(w_down.astype(jnp.bfloat16), 'dp', axis=1, tiled=True)  215 us
    reduce_scatter x1, waiting for transfers between devices, per_device(): lax.psum_scatter(grad_gate.astype(jnp.bfloat16), 'dp', scatter_dimension=...  199 us
    reduce_scatter x1, waiting for transfers between devices, per_device(): lax.psum_scatter(grad_value_mat, ('dp', 'expert'), scatter_dimension=0, t...  188 us
    reduce_scatter x1, waiting for transfers between devices, per_device(): lax.psum_scatter(grad_query_mat, ('dp', 'expert'), scatter_dimension=0, t...  187 us
    all_gather x1, waiting for transfers between devices, per_device(): lax.all_gather(w_up.astype(jnp.bfloat16), 'dp', axis=1, tiled=True)  187 us
    reduce_scatter x1, waiting for transfers between devices, per_device(): lax.psum_scatter(grad_key_mat, ('dp', 'expert'), scatter_dimension=0, til...  186 us
  transfers between devices with their start and end apart: 29, of which 18 were waited for; matrix products, arithmetic and copies ran while one was open for 11% of the time, Pallas kernels for 0%

profile of v1, /device:TPU:3, one launch (start us, length us, event | category | flops | bytes accessed | tf_op | source)
XLA Modules:
  0.0 3074.1 jit_solution(8459145906041783301)
XLA Ops:
  24.1 6.7 broadcast_in_dim.62
  49.2 87.8 %collective-permute-done = bf16[4,256,1024]{2,1,0:T(8,128)(2,1)} collective-permute-done((bf16[4,256,1024]{2,1,0:T(8,128)(2,1)}, bf16[4,256,1024]{2,1,0:T(8,128)(2,1)}, u32[]{:S(2)}, u32[]{:S(2)}) %collective-permute-start) | collective-permute-done | bytes 2097184 | tf_op jit(solution)/shard_map/ppermute | solution.py:19
  149.4 6.8 gather_fusion.3
  156.2 6.7 select_convert_fusion
  162.9 9.9 all-to-all-start.2
  174.0 67.0 %collective-permute-done.2 = bf16[4,256,1024]{2,1,0:T(8,128)(2,1)} collective-permute-done((bf16[4,256,1024]{2,1,0:T(8,128)(2,1)}, bf16[4,256,1024]{2,1,0:T(8,128)(2,1)}, u32[]{:S(2)}, u32[]{:S(2)}) %collective-permute-start.2) | collective-permute-done | bytes 2097184 | tf_op jit(solution)/shard_map/ppermute | solution.py:19
  248.0 79.3 %all-gather.20.cloned.1.call-done = bf16[2048,2048]{1,0:T(8,128)(2,1)} async-done(((bf16[64,2048]{1,0:T(8,128)(2,1)}), bf16[2048,2048]{1,0:T(8,128)(2,1)}) %all-gather.20.cloned.1.call-update) | async-done | bytes 8388624 | tf_op jit(solution)/shard_map/all_gather | solution.py:119
  340.0 67.0 %all-gather.16.cloned.1.call-done = bf16[2048,2048]{1,0:T(8,128)(2,1)} async-done(((bf16[64,2048]{1,0:T(8,128)(2,1)}), bf16[2048,2048]{1,0:T(8,128)(2,1)}) %all-gather.16.cloned.1.call-update) | async-done | bytes 8388624 | tf_op jit(solution)/shard_map/all_gather | solution.py:120
  415.1 71.5 %all-gather.22.cloned.1.call-done = bf16[2048,2048]{1,0:T(8,128)(2,1)} async-done(((bf16[64,2048]{1,0:T(8,128)(2,1)}), bf16[2048,2048]{1,0:T(8,128)(2,1)}) %all-gather.22.cloned.1.call-update) | async-done | bytes 8388624 | tf_op jit(solution)/shard_map/all_gather | solution.py:121
  491.5 5.9 gather_fusion
  526.0 87.1 %collective-permute-done.5 = bf16[4,256,1024]{2,1,0:T(8,128)(2,1)} collective-permute-done((bf16[4,256,1024]{2,1,0:T(8,128)(2,1)}, bf16[4,256,1024]{2,1,0:T(8,128)(2,1)}, u32[]{:S(2)}, u32[]{:S(2)}) %collective-permute-start.5) | collective-permute-done | bytes 2097184 | tf_op jit(solution)/shard_map/ppermute | solution.py:22
  616.2 5.9 copy.102
  630.5 127.9 %all-gather.24.cloned.1.call-done = bf16[4,2048,1024]{2,1,0:T(8,128)(2,1)} async-done(((bf16[4,256,1024]{2,1,0:T(8,128)(2,1)}), bf16[4,2048,1024]{2,1,0:T(8,128)(2,1)}) %all-gather.24.cloned.1.call-update) | async-done | bytes 16777232 | tf_op jit(solution)/shard_map/all_gather | solution.py:171
  758.4 13.1 fusion.79
  771.5 215.5 %all-gather.26.cloned.1.call-done = bf16[4,1024,2048]{2,1,0:T(8,128)(2,1)} async-done(((bf16[4,128,2048]{2,1,0:T(8,128)(2,1)}), bf16[4,1024,2048]{2,1,0:T(8,128)(2,1)}) %all-gather.26.cloned.1.call-update) | async-done | bytes 16777232 | tf_op jit(solution)/shard_map/all_gather | solution.py:173
  987.0 11.7 fusion.80
  998.6 17.8 multiply_convert_fusion
  1016.4 11.5 fusion.81
  1028.0 187.0 %all-gather.30.cloned.1.call-done = bf16[4,2048,1024]{2,1,0:T(8,128)(2,1)} async-done(((bf16[4,256,1024]{2,1,0:T(8,128)(2,1)}), bf16[4,2048,1024]{2,1,0:T(8,128)(2,1)}) %all-gather.30.cloned.1.call-update) | async-done | bytes 16777232 | tf_op jit(solution)/shard_map/all_gather | solution.py:194
  1215.0 13.7 fusion.2
  1228.7 8.1 copy.103
  1236.8 6.4 all-to-all-start.3
  1243.2 11.5 convert_bitcast_fusion
  1254.7 5.8 copy.99
  1260.4 35.8 %all-to-all-done.3 = bf16[1,4,288,2048]{3,1,0,2:T(4,128)(2,1)} async-done(((bf16[1,4,288,2048]{3,1,0,2:T(4,128)(2,1)}), bf16[1,4,288,2048]{3,1,0,2:T(4,128)(2,1)}, u32[]{:S(2)}, u32[]{:S(2)}) %all-to-all-start.3) | async-done | bytes 4718624 | tf_op jit(solution)/shard_map/all_to_all | solution.py:230
  1296.2 5.9 all-to-all-start.1
  1302.2 7.1 copy.104
  1309.3 11.9 gather_fusion.4
  1326.6 28.4 all-to-all-done.1
  1355.1 7.0 copy.100
  1362.1 11.9 gather_fusion.1
  1374.1 6.5 fusion.1
  1382.9 7.2 convolution_convert_fusion.3
  1414.5 14.7 convolution_convert_fusion.2
  1429.3 14.9 convolution_convert_fusion.1
  1444.3 15.4 convolution_convert_fusion
  1459.8 9.1 fusion.37
  1470.0 8.2 fusion.28
  1479.2 8.3 fusion.67
  1488.5 8.3 fusion.69
  1500.0 42.2 %all-reduce.4 = (f32[2048]{0:T(1024)S(1)}, f32[2048]{0:T(1024)S(1)}, f32[2048]{0:T(1024)S(1)}, f32[2048]{0:T(1024)S(1)}) all-reduce(f32[2048]{0:T(1024)S(1)} %get-tuple-element.13, f32[2048]{0:T(1024)S(1)} %get-tuple-element.19, f32[2048]{0:T(1024)S(1)} %get-tuple-element.17, ...), channel_id=4, replica_groups=mesh['dp'=8,'expert'=4] {'dp','expert'}, use_global_device_ids=true, to_apply=%region_20.21.clone | all-reduce | flops 8192 | bytes 65536
  1548.4 198.7 %reduce-scatter.16.cloned.1.call-done = bf16[4,256,1024]{2,1,0:T(8,128)(2,1)} async-done(((bf16[4,2048,1024]{2,1,0:T(8,128)(2,1)}), bf16[4,256,1024]{2,1,0:T(8,128)(2,1)}) %reduce-scatter.16.cloned.1.call-update) | async-done | bytes 2097168 | tf_op jit(solution)/shard_map/reduce_scatter | solution.py:220
  1751.2 281.9 %reduce-scatter.18.cloned.1.call-done = bf16[4,256,1024]{2,1,0:T(8,128)(2,1)} async-done(((bf16[4,2048,1024]{2,1,0:T(8,128)(2,1)}), bf16[4,256,1024]{2,1,0:T(8,128)(2,1)}) %reduce-scatter.18.cloned.1.call-update) | async-done | bytes 2097168 | tf_op jit(solution)/shard_map/reduce_scatter | solution.py:223
  2037.2 281.2 %reduce-scatter.20.cloned.1.call-done = bf16[4,128,2048]{2,1,0:T(8,128)(2,1)} async-done(((bf16[4,1024,2048]{2,1,0:T(8,128)(2,1)}), bf16[4,128,2048]{2,1,0:T(8,128)(2,1)}) %reduce-scatter.20.cloned.1.call-update) | async-done | bytes 2097168 | tf_op jit(solution)/shard_map/reduce_scatter | solution.py:226
  2322.6 182.7 %reduce-scatter.14.cloned.1.call-done = f32[64,2048]{1,0:T(8,128)} async-done(((f32[2048,2048]{1,0:T(8,128)}), f32[64,2048]{1,0:T(8,128)}) %reduce-scatter.14.cloned.1.call-update) | async-done | bytes 524304 | tf_op jit(solution)/shard_map/reduce_scatter | solution.py:294
  2505.3 187.8 %reduce-scatter.12.cloned.1.call-done = f32[64,2048]{1,0:T(8,128)} async-done(((f32[2048,2048]{1,0:T(8,128)}), f32[64,2048]{1,0:T(8,128)}) %reduce-scatter.12.cloned.1.call-update) | async-done | bytes 524304 | tf_op jit(solution)/shard_map/reduce_scatter | solution.py:293
  2693.1 186.5 %reduce-scatter.10.cloned.1.call-done = f32[64,2048]{1,0:T(8,128)} async-done(((f32[2048,2048]{1,0:T(8,128)}), f32[64,2048]{1,0:T(8,128)}) %reduce-scatter.10.cloned.1.call-update) | async-done | bytes 524304 | tf_op jit(solution)/shard_map/reduce_scatter | solution.py:292
  2879.6 187.4 %reduce-scatter.8.cloned.1.call-done = f32[64,2048]{1,0:T(8,128)} async-done(((f32[2048,2048]{1,0:T(8,128)}), f32[64,2048]{1,0:T(8,128)}) %reduce-scatter.8.cloned.1.call-update) | async-done | bytes 524304 | tf_op jit(solution)/shard_map/reduce_scatter | solution.py:291
  (272 shorter events, 174.1 us)
Async XLA Ops:
  7.2 141.1 %all-gather.28.cloned.1.call-start = ((), (), s32[]{:S(2)}) async-start(), calls=%async_computation.18 | async-start | bytes 2621440 | tf_op jit(solution)/shard_map/all_gather | solution.py:106
  7.9 164.8 %all-gather.14.cloned.1.call-start = ((), (), s32[]{:S(2)}) async-start(), calls=%async_computation.11 | async-start | bytes 2621440 | tf_op jit(solution)/shard_map/all_gather | solution.py:105
  8.7 233.0 %all-gather.18.cloned.1.call-start = ((), (), s32[]{:S(2)}) async-start(), calls=%async_computation.13 | async-start | bytes 8650752 | tf_op jit(solution)/shard_map/all_gather | solution.py:118
  10.5 316.8 %all-gather.20.cloned.1.call-start = ((), (), s32[]{:S(2)}) async-start(), calls=%async_computation.14 | async-start | bytes 8650752 | tf_op jit(solution)/shard_map/all_gather | solution.py:119
  12.4 394.7 %all-gather.16.cloned.1.call-start = ((), (), s32[]{:S(2)}) async-start(), calls=%async_computation.12 | async-start | bytes 8650752 | tf_op jit(solution)/shard_map/all_gather | solution.py:120
  14.2 472.3 %all-gather.22.cloned.1.call-start = ((), (), s32[]{:S(2)}) async-start(), calls=%async_computation.15 | async-start | bytes 8650752 | tf_op jit(solution)/shard_map/all_gather | solution.py:121
  16.1 742.4 %all-gather.24.cloned.1.call-start = ((), (), s32[]{:S(2)}) async-start(), calls=%async_computation.16 | async-start | bytes 18874368 | tf_op jit(solution)/shard_map/all_gather | solution.py:171
  20.2 966.8 %all-gather.26.cloned.1.call-start = ((), (), s32[]{:S(2)}) async-start(), calls=%async_computation.17 | async-start | bytes 18874368 | tf_op jit(solution)/shard_map/all_gather | solution.py:173
  24.1 1190.9 %all-gather.30.cloned.1.call-start = ((), (), s32[]{:S(2)}) async-start(), calls=%async_computation.19 | async-start | bytes 18874368 | tf_op jit(solution)/shard_map/all_gather | solution.py:194
  30.8 106.4 %copy-start.47 = (s32[1,4]{1,0:T(1,128)S(1)}, s32[1,4]{1,0:T(1,128)}, u32[]{:S(2)}) copy-start(s32[1,4]{1,0:T(1,128)} %param.20) | copy-start | bytes 52
  30.8 108.3 %copy-start.34 = (f32[1,128,8]{1,2,0:T(8,128)S(1)}, f32[1,128,8]{1,2,0:T(8,128)}, u32[]{:S(2)}) copy-start(f32[1,128,8]{1,2,0:T(8,128)} %param.22) | copy-start | bytes 12292
  33.5 103.5 %collective-permute-start = (bf16[4,256,1024]{2,1,0:T(8,128)(2,1)}, bf16[4,256,1024]{2,1,0:T(8,128)(2,1)}, u32[]{:S(2)}, u32[]{:S(2)}) collective-permute-start(bf16[4,256,1024]{2,1,0:T(8,128)(2,1)} %get-tuple-element.26), channel_id=1, source_target_pairs={{0,4},{4,8},{8,12},{12,16},{16,20},{20,24},{24,28},{28,0},{1,5},{5... | collective-permute-start | bytes 6291464 | tf_op jit(solution)/shard_map/ppermute | solution.py:19
  34.8 112.2 %collective-permute-start.1 = (bf16[4,256,1024]{2,1,0:T(8,128)(2,1)}, bf16[4,256,1024]{2,1,0:T(8,128)(2,1)}, u32[]{:S(2)}, u32[]{:S(2)}) collective-permute-start(bf16[4,256,1024]{2,1,0:T(8,128)(2,1)} %get-tuple-element.26), channel_id=1, source_target_pairs={{0,28},{4,0},{8,4},{12,8},{16,12},{20,16},{24,20},{28,24},{1,29},{... | collective-permute-start | bytes 6291464 | tf_op jit(solution)/shard_map/ppermute | solution.py:22
  35.3 109.4 %copy-start.46 = (s32[4]{0:T(128)S(1)}, s32[4]{0:T(128)}, u32[]{:S(2)}) copy-start(s32[4]{0:T(128)} %param.19) | copy-start | bytes 52
  40.5 107.8 %copy-start.37 = (s32[1024,1]{0,1:T(1,128)}, s32[1024,1]{0,1:T(1,128)S(1)}, u32[]{:S(2)}) copy-start(s32[1024,1]{0,1:T(1,128)S(1)} %compare_select_fusion) | copy-start | bytes 12292
  137.0 103.9 %collective-permute-start.2 = (bf16[4,256,1024]{2,1,0:T(8,128)(2,1)}, bf16[4,256,1024]{2,1,0:T(8,128)(2,1)}, u32[]{:S(2)}, u32[]{:S(2)}) collective-permute-start(bf16[4,256,1024]{2,1,0:T(8,128)(2,1)} %collective-permute-done), channel_id=1, source_target_pairs={{0,4},{4,8},{8,12},{12,16},{16,20},{20,24},{24,28},{28,0},{1,5},{5... | collective-permute-start | bytes 6291464 | tf_op jit(solution)/shard_map/ppermute | solution.py:19
  146.0 266.6 %copy-start.39 = (pred[128,128]{0,1:T(8,128)(4,1)}, pred[128,128]{0,1:T(8,128)(4,1)S(1)}, u32[]{:S(2)}) copy-start(pred[128,128]{0,1:T(8,128)(4,1)S(1)} %fusion.48) | copy-start | bytes 49156
  146.9 187.2 %copy-start.24 = (f32[128,64]{1,0:T(8,128)}, f32[128,64]{1,0:T(8,128)S(1)}, u32[]{:S(2)}) copy-start(f32[128,64]{1,0:T(8,128)S(1)} %get-tuple-element.52) | copy-start | bytes 98308
  146.9 361.1 %collective-permute-start.3 = (bf16[4,256,1024]{2,1,0:T(8,128)(2,1)}, bf16[4,256,1024]{2,1,0:T(8,128)(2,1)}, u32[]{:S(2)}, u32[]{:S(2)}) collective-permute-start(bf16[4,256,1024]{2,1,0:T(8,128)(2,1)} %collective-permute-done.1), channel_id=1, source_target_pairs={{0,28},{4,0},{8,4},{12,8},{16,12},{20,16},{24,20},{28,24},{1,29},{... | collective-permute-start | bytes 6291464 | tf_op jit(solution)/shard_map/ppermute | solution.py:22
  162.9 78.8 %copy-start.13 = (f32[2048]{0:T(1024)S(1)}, f32[2048]{0:T(1024)}, u32[]{:S(2)}) copy-start(f32[2048]{0:T(1024)} %param.23) | copy-start | bytes 24580
  162.9 340.0 %all-to-all-start.2 = ((bf16[4,4,72,2048]{3,2,1,0:T(8,128)(2,1)}), bf16[4,4,72,2048]{3,2,1,0:T(8,128)(2,1)}, u32[]{:S(2)}, u32[]{:S(2)}) async-start(bf16[4,4,72,2048]{3,2,1,0:T(8,128)(2,1)} %select_convert_fusion), calls=%async_computation.2 | async-start | bytes 9437184 | tf_op jit(solution)/shard_map/all_to_all | solution.py:191
  174.0 233.1 %copy-start.27 = (f32[128]{0:T(128)}, f32[128]{0:T(128)S(1)}, u32[]{:S(2)}) copy-start(f32[128]{0:T(128)S(1)} %add_rsqrt_fusion.3) | copy-start | bytes 1540
  174.0 73.7 %copy-start.32 = (f32[2048]{0:T(1024)S(1)}, f32[2048]{0:T(1024)}, u32[]{:S(2)}) copy-start(f32[2048]{0:T(1024)} %param.27) | copy-start | bytes 24580
  174.0 153.3 %copy-start.4 = (bf16[4,128,2048]{2,1,0:T(8,128)(2,1)S(1)}, bf16[4,128,2048]{2,1,0:T(8,128)(2,1)}, u32[]{:S(2)}) copy-start(bf16[4,128,2048]{2,1,0:T(8,128)(2,1)} %all-gather.14.cloned.1.call-done) | copy-start | bytes 6291460
  241.0 267.5 %collective-permute-start.4 = (bf16[4,256,1024]{2,1,0:T(8,128)(2,1)}, bf16[4,256,1024]{2,1,0:T(8,128)(2,1)}, u32[]{:S(2)}, u32[]{:S(2)}) collective-permute-start(bf16[4,256,1024]{2,1,0:T(8,128)(2,1)} %collective-permute-done.2), channel_id=1, source_target_pairs={{0,4},{4,8},{8,12},{12,16},{16,20},{20,24},{24,28},{28,0},{1,5},{5... | collective-permute-start | bytes 6291464 | tf_op jit(solution)/shard_map/ppermute | solution.py:19
  248.0 85.1 %copy-start.30 = (f32[2048]{0:T(1024)S(1)}, f32[2048]{0:T(1024)}, u32[]{:S(2)}) copy-start(f32[2048]{0:T(1024)} %param.28) | copy-start | bytes 24580
  336.5 76.1 %copy-start.15 = (bf16[128,16,64]{2,0,1:T(8,128)(2,1)}, bf16[128,16,64]{2,0,1:T(8,128)(2,1)S(1)}, u32[]{:S(2)}) copy-start(bf16[128,16,64]{2,0,1:T(8,128)(2,1)S(1)} %get-tuple-element.30) | copy-start | bytes 786436
  336.5 76.1 %copy-start.17 = (bf16[128,16,64]{2,0,1:T(8,128)(2,1)}, bf16[128,16,64]{2,0,1:T(8,128)(2,1)S(1)}, u32[]{:S(2)}) copy-start(bf16[128,16,64]{2,0,1:T(8,128)(2,1)S(1)} %get-tuple-element.31) | copy-start | bytes 786436
  340.0 72.6 %copy-start.40 = (f32[16,128]{1,0:T(8,128)}, f32[16,128]{1,0:T(8,128)S(1)}, u32[]{:S(2)}) copy-start(f32[16,128]{1,0:T(8,128)S(1)} %get-tuple-element.57) | copy-start | bytes 24580
  415.1 76.3 %copy-start.12 = (bf16[16,128,128]{2,1,0:T(8,128)(2,1)}, bf16[16,128,128]{2,1,0:T(8,128)(2,1)S(1)}, u32[]{:S(2)}) copy-start(bf16[16,128,128]{2,1,0:T(8,128)(2,1)S(1)} %convolution_convert_fusion.6) | copy-start | bytes 1572868
  502.9 122.5 %all-to-all-start = ((bf16[4,4,72,2048]{3,2,1,0:T(8,128)(2,1)}), bf16[4,4,72,2048]{3,2,1,0:T(8,128)(2,1)}, u32[]{:S(2)}, u32[]{:S(2)}) async-start(bf16[4,4,72,2048]{3,2,1,0:T(8,128)(2,1)} %broadcast_select_fusion), calls=%async_computation | async-start | bytes 9437184 | tf_op jit(solution)/shard_map/all_to_all | solution.py:169
  508.1 105.0 %collective-permute-start.5 = (bf16[4,256,1024]{2,1,0:T(8,128)(2,1)}, bf16[4,256,1024]{2,1,0:T(8,128)(2,1)}, u32[]{:S(2)}, u32[]{:S(2)}) collective-permute-start(bf16[4,256,1024]{2,1,0:T(8,128)(2,1)} %collective-permute-done.3), channel_id=1, source_target_pairs={{0,28},{4,0},{8,4},{12,8},{16,12},{20,16},{24,20},{28,24},{1,29},{... | collective-permute-start | bytes 6291464 | tf_op jit(solution)/shard_map/ppermute | solution.py:22
  508.5 113.6 %collective-permute-start.6 = (bf16[4,256,1024]{2,1,0:T(8,128)(2,1)}, bf16[4,256,1024]{2,1,0:T(8,128)(2,1)}, u32[]{:S(2)}, u32[]{:S(2)}) collective-permute-start(bf16[4,256,1024]{2,1,0:T(8,128)(2,1)} %collective-permute-done.4), channel_id=1, source_target_pairs={{0,4},{4,8},{8,12},{12,16},{16,20},{20,24},{24,28},{28,0},{1,5},{5... | collective-permute-start | bytes 6291464 | tf_op jit(solution)/shard_map/ppermute | solution.py:19
  987.0 11.7 copy-start.8
  1236.8 59.4 %all-to-all-start.3 = ((bf16[1,4,288,2048]{3,1,0,2:T(4,128)(2,1)}), bf16[1,4,288,2048]{3,1,0,2:T(4,128)(2,1)}, u32[]{:S(2)}, u32[]{:S(2)}) async-start(bf16[1,4,288,2048]{3,1,0,2:T(4,128)(2,1)} %copy.103), calls=%async_computation.3 | async-start | bytes 9437184 | tf_op jit(solution)/shard_map/all_to_all | solution.py:230
  1260.4 41.6 %copy-start.35 = (f32[1,128,8]{1,2,0:T(8,128)S(1)}, f32[1,128,8]{1,2,0:T(8,128)}, u32[]{:S(2)}) copy-start(f32[1,128,8]{1,2,0:T(8,128)} %param.22) | copy-start | bytes 12292
  1260.4 41.7 %copy-start.38 = (s32[1024,1]{0,1:T(1,128)S(1)}, s32[1024,1]{0,1:T(1,128)}, u32[]{:S(2)}) copy-start(s32[1024,1]{0,1:T(1,128)} %copy-done.37) | copy-start | bytes 12292
  1296.2 58.9 %all-to-all-start.1 = ((bf16[1,4,288,2048]{3,1,0,2:T(4,128)(2,1)}), bf16[1,4,288,2048]{3,1,0,2:T(4,128)(2,1)}, u32[]{:S(2)}, u32[]{:S(2)}) async-start(bf16[1,4,288,2048]{3,1,0,2:T(4,128)(2,1)} %copy.99), calls=%async_computation.1 | async-start | bytes 9437184 | tf_op jit(solution)/shard_map/all_to_all | solution.py:180
  1302.0 242.6 %all-gather.34.cloned.1.call-start = ((), (), s32[]{:S(2)}) async-start(), calls=%async_computation.28 | async-start | bytes 2621440 | tf_op jit(solution)/shard_map/all_gather | solution.py:302
  1382.9 9.3 copy-start.41
  1413.7 132.8 %all-gather.32.cloned.1.call-start = ((), (), s32[]{:S(2)}) async-start(), calls=%async_computation.27 | async-start | bytes 2621440 | tf_op jit(solution)/shard_map/all_gather | solution.py:301
  1414.4 332.7 %reduce-scatter.16.cloned.1.call-start = ((), (), s32[]{:S(2)}) async-start(), calls=%async_computation.24 | async-start | bytes 18874368 | tf_op jit(solution)/shard_map/reduce_scatter | solution.py:220
  1429.2 603.9 %reduce-scatter.18.cloned.1.call-start = ((), (), s32[]{:S(2)}) async-start(), calls=%async_computation.25 | async-start | bytes 18874368 | tf_op jit(solution)/shard_map/reduce_scatter | solution.py:223
  1444.3 874.2 %reduce-scatter.20.cloned.1.call-start = ((), (), s32[]{:S(2)}) async-start(), calls=%async_computation.26 | async-start | bytes 18874368 | tf_op jit(solution)/shard_map/reduce_scatter | solution.py:226
  1459.7 1045.6 %reduce-scatter.14.cloned.1.call-start = ((), (), s32[]{:S(2)}) async-start(), calls=%async_computation.23 | async-start | bytes 17301504 | tf_op jit(solution)/shard_map/reduce_scatter | solution.py:294
  1468.9 1224.2 %reduce-scatter.12.cloned.1.call-start = ((), (), s32[]{:S(2)}) async-start(), calls=%async_computation.22 | async-start | bytes 17301504 | tf_op jit(solution)/shard_map/reduce_scatter | solution.py:293
  1478.2 1401.4 %reduce-scatter.10.cloned.1.call-start = ((), (), s32[]{:S(2)}) async-start(), calls=%async_computation.21 | async-start | bytes 17301504 | tf_op jit(solution)/shard_map/reduce_scatter | solution.py:292
  1487.5 1579.6 %reduce-scatter.8.cloned.1.call-start = ((), (), s32[]{:S(2)}) async-start(), calls=%async_computation.20 | async-start | bytes 17301504 | tf_op jit(solution)/shard_map/reduce_scatter | solution.py:291
  (36 other events, 118.5 us)
Sparse Core Ops, SparseCore 0:
  9.6 24.2 all-gather.27
  35.4 22.5 all-gather.13
  61.5 156.5 all-gather.17
  221.4 105.9 all-gather.19
  330.6 76.4 all-gather.15
  410.4 76.1 all-gather.21
  489.3 269.0 all-gather.23
  761.2 225.7 all-gather.25
  989.2 225.7 all-gather.29
  1413.8 21.3 all-gather.33
  1437.4 22.5 all-gather.31
  1463.6 283.4 reduce-scatter.15
  1751.4 281.6 reduce-scatter.17
  2036.8 281.6 reduce-scatter.19
  2321.2 183.9 reduce-scatter.13
  2508.1 184.9 reduce-scatter.11
  2695.9 183.6 reduce-scatter.9
  2882.4 184.5 reduce-scatter.7
